TPU v7x, 256 devices: a whole 4x4x8 slice. The times are simulated.
256 devices in a mesh: order: 64 (over z, x, core), lat: 4 (over y).
Axes of the slice: x: 4, y: 4, z: 8, core: 2. Of those that a mesh axis runs over, the one named last changes fastest.
Arguments:
- position: float32 [128, 2, 64, 2160], P('order', None, None, 'lat'), may hold values from -6 to 6
- residual: float32 [128, 2, 64, 2160], P('order', None, None, 'lat'), as said below
- direction: float32 [128, 2, 64, 2160], P('order', None, None, 'lat'), as said below
- legendre: float32 [128, 2160, 2048], P('order', None, 'lat'), may hold values from -0.125 to 0.125
- order_of: int32 [128], replicated, may hold values from 0 to 2032, as said below
- class_idx: int32 [2048, 4320], P(('lat', 'order')), may hold values from 0 to 15
- land: int32 [2048, 4320], P(('lat', 'order')), may hold values 0 or 1
- class_weight: float32 [16, 2], replicated, may hold values from 0.2 to 5
- damping: float32 [2160], P('lat'), may hold values from 0.05 to 0.5
Outputs:
- new_position: float32 [128, 2, 64, 2160], P('order', None, None, 'lat')
- new_residual: float32 [128, 2, 64, 2160], P('order', None, None, 'lat')
- new_direction: float32 [128, 2, 64, 2160], P('order', None, None, 'lat')
Inputs may be any that keep to these rules, and one draw needn't show every extreme that they name: `order_of`: distinct multiples of 16: each of 0, 16, ..., 16 * (128 - 1) appears exactly once. `residual`: real-valued and not zero. `direction`: real-valued and not zero.
All inputs are finite; a program needn't handle non-finite values. No bound on the sum of `land` on one device may be relied on, other than what follows from the above.
Results may differ from a plain program's by a relative error of at most 0.000058.
Values sent between devices are 32-bit elements; how exact they have to be, the bound alone decides.
A program may use at most 128 MiB of HBM per device.

v0:
```python
import math
import jax
import jax.numpy as jnp
from jax import lax
from jax.sharding import PartitionSpec as P


def tables(order_of, longitudes):
    longitude = jnp.arange(longitudes, dtype=jnp.int32)
    phases = order_of[:, None] * longitude[None, :] % longitudes
    angles = phases.astype(jnp.float32) * (2.0 * math.pi / longitudes)
    return jnp.stack([jnp.cos(angles), jnp.sin(angles)])


def sample_sums(product):
    return jnp.sum(product, axis=(0, 1, 3))


def shards(
    position, residual, direction, legendre, order_of, class_idx, land, class_weight, damping
):
    highest = lax.Precision.HIGHEST
    m_local = position.shape[0]
    samples = position.shape[2]
    deg_local = position.shape[3]
    band_rows = legendre.shape[2]
    lat_index = lax.axis_index("lat")
    order_index = lax.axis_index("order")
    my_orders = lax.dynamic_slice_in_dim(order_of, order_index * m_local, m_local)
    deg_start = lat_index * deg_local
    own_degrees = deg_start + jnp.arange(deg_local, dtype=jnp.int32)
    own_valid = (own_degrees[None, :] >= my_orders[:, None]).astype(jnp.float32)[:, None, None, :]
    pos_m = position * own_valid
    res_m = residual * own_valid
    dir_m = direction * own_valid
    norm_before = lax.psum(sample_sums(res_m * res_m), ("order", "lat"))
    block_part = lax.all_gather(direction, "lat", axis=3, tiled=True)
    degree_count = block_part.shape[3]
    in_block = jnp.arange(degree_count, dtype=jnp.int32)
    in_triangle = (in_block[None, :] >= my_orders[:, None]).astype(jnp.float32)
    masked = block_part * in_triangle[:, None, None, :]
    synthesis = jnp.einsum("mskd,mdt->mtsk", masked, legendre, precision=highest)
    grid_in = lax.all_to_all(
        synthesis.reshape(m_local, band_rows, 2 * samples),
        "order",
        split_axis=1,
        concat_axis=0,
        tiled=True,
    )
    orders_all = grid_in.shape[0]
    rows_here = grid_in.shape[1]
    grid_in = grid_in.reshape(orders_all, rows_here, 2, samples)
    longitudes = class_idx.shape[1]
    harmonic = tables(order_of, longitudes)
    surface = jnp.einsum("mrsk,sml->rkl", grid_in, harmonic, precision=highest)
    class_count = class_weight.shape[0]
    onehot = (
        class_idx[:, :, None] == jnp.arange(class_count, dtype=jnp.int32)[None, None, :]
    ).astype(jnp.float32)
    by_class = jnp.dot(onehot, class_weight, precision=highest)
    weight_grid = jnp.where(land == 1, by_class[:, :, 1], by_class[:, :, 0])
    weighted = surface * weight_grid[:, None, :]
    spectra = jnp.einsum("rkl,sml->mrsk", weighted, harmonic, precision=highest) * (
        2.0 / longitudes
    )
    returned = lax.all_to_all(
        spectra.reshape(orders_all, rows_here, 2 * samples),
        "order",
        split_axis=0,
        concat_axis=1,
        tiled=True,
    )
    returned = returned.reshape(m_local, band_rows, 2, samples)
    band_part = jnp.einsum("mtsk,mdt->mskd", returned, legendre, precision=highest)
    totals = lax.psum(band_part, "lat")
    summed = lax.dynamic_slice_in_dim(totals, deg_start, deg_local, 3)
    applied = (summed + damping[None, None, None, :] * dir_m) * own_valid
    curvature_sum = lax.psum(sample_sums(dir_m * applied), ("order", "lat"))
    step_size = (norm_before / curvature_sum)[None, None, :, None]
    new_residual = res_m - step_size * applied
    norm_after = lax.psum(sample_sums(new_residual * new_residual), ("order", "lat"))
    ratio_new = (norm_after / norm_before)[None, None, :, None]
    new_position = pos_m + step_size * dir_m
    new_direction = new_residual + ratio_new * dir_m
    return (new_position, new_residual, new_direction)


def solution(mesh):
    return jax.shard_map(
        shards,
        mesh=mesh,
        in_specs=(
            P("order", None, None, "lat"),
            P("order", None, None, "lat"),
            P("order", None, None, "lat"),
            P("order", None, "lat"),
            P(),
            P(("lat", "order"), None),
            P(("lat", "order"), None),
            P(),
            P("lat"),
        ),
        out_specs=(
            P("order", None, None, "lat"),
            P("order", None, None, "lat"),
            P("order", None, None, "lat"),
        ),
        check_vma=False,
    )
```

profile of v0, /device:TPU:1, one launch (start us, length us, event | category | flops | bytes accessed | tf_op | source)
XLA Modules:
  0.0 419.9 jit_solution(14200132624685688203)
XLA Ops:
  7.2 2.3 copy.20
  9.7 0.7 fusion.11
  10.6 0.9 fusion.37
  11.4 9.9 %fusion.17 = (f32[1,128,4320]{1,2,0:T(8,128)S(1)}, f32[1,128,4320]{1,2,0:T(8,128)}) fusion(s32[128]{0:T(128)S(1)} %copy-done.10), kind=kLoop, calls=%fused_computation.23 | loop fusion | flops 4976640 | bytes 4424192 | tf_op jit(solution)/shard_map/cos | solution.py:12
  21.3 44.9 %all-gather.2.cloned.1.call-done = f32[2,2,64,2160]{2,1,0,3:T(2,128)} async-done(((f32[2,2,64,540]{2,1,0,3:T(2,128)}), f32[2,2,64,2160]{2,1,0,3:T(2,128)}) %all-gather.2.cloned.1.call-update) | async-done | bytes 2211856 | tf_op jit(solution)/shard_map/all_gather | solution.py:37
  66.2 6.6 %broadcast_multiply_fusion = f32[2,2,64,2160]{2,1,0,3:T(2,128)S(1)} fusion(f32[2,2,64,2160]{2,1,0,3:T(2,128)} %all-gather.2.cloned.1.call-done, f32[2,2160]{0,1:T(8,128)S(1)} %fusion.30), kind=kLoop, calls=%fused_computation.18 | loop fusion | flops 552960 | bytes 4440960 | tf_op jit(solution)/shard_map/mul | solution.py:41
  72.8 8.7 %fusion.4 = f32[2,2,64,512]{3,2,1,0:T(8,128)S(1)} fusion(f32[2,2160,512]{2,1,0:T(8,128)S(1)} %copy-done.1, f32[2,2,64,2160]{2,1,0,3:T(2,128)S(1)} %broadcast_multiply_fusion), kind=kOutput, calls=%fused_computation.5 | convolution fusion | flops 3397386240 | bytes 11583488 | tf_op jit(solution)/shard_map/mskd,mdt->mtsk/dot_general | solution.py:42
  81.5 1.0 copy.22
  82.5 10.8 %all-to-all-start = ((f32[2,512,128]{2,0,1:T(2,128)}), f32[2,512,128]{2,0,1:T(2,128)S(1)}, u32[]{:S(2)}, u32[]{:S(2)}) async-start(f32[2,512,128]{2,0,1:T(2,128)} %copy.22), calls=%async_computation | async-start | bytes 1048576 | tf_op jit(solution)/shard_map/all_to_all | solution.py:43
  93.6 17.4 %all-to-all-done = f32[2,512,128]{2,0,1:T(2,128)S(1)} async-done(((f32[2,512,128]{2,0,1:T(2,128)}), f32[2,512,128]{2,0,1:T(2,128)S(1)}, u32[]{:S(2)}, u32[]{:S(2)}) %all-to-all-start) | async-done | bytes 524320 | tf_op jit(solution)/shard_map/all_to_all | solution.py:43
  111.0 0.8 copy.24
  111.9 1.6 reshape.148
  113.5 31.3 %fusion.8 = f32[8,64,4320,1]{2,1,3,0:T(8,128)S(1)} fusion(f32[1,128,4320]{1,2,0:T(8,128)} %get-tuple-element.13, f32[1,128,4320]{1,2,0:T(8,128)S(1)} %get-tuple-element.12, f32[128,8,2,64]{3,2,1,0:T(2,128)S(1)} %reshape.148), kind=kOutput, calls=%fused_computation.10 | convolution fusion | flops 6795878400 | bytes 13795328 | tf_op jit(solution)/shard_map/mrsk,sml->rkl/dot_general | solution.py:55
  144.8 7.8 %fusion.24 = f32[128,8,2,64]{0,3,1,2:T(8,128)S(1)} fusion(f32[8,64,4320,1]{2,1,3,0:T(8,128)S(1)} %fusion.8, f32[8,4320]{1,0:T(8,128)S(1)} %fusion.33, f32[1,128,4320]{1,2,0:T(8,128)S(1)} %copy-done.2, f32[1,128,4320]{1,2,0:T(8,128)S(1)} %get-tuple-element.12), kind=kOutput, calls=%fused_computation.26 | convolution fusion | flops 6798221312 | bytes 13933568 | tf_op jit(solution)/shard_map/rkl,sml->mrsk/dot_general | solution.py:63
  152.7 0.2 copy.28
  153.0 23.3 %all_to_all.30 = f32[128,8,128]{2,1,0:T(8,128)S(1)} all-to-all(f32[128,8,128]{2,1,0:T(8,128)S(1)} %copy.28), channel_id=1, replica_groups=mesh['order'=64,'lat'=4] {'order'}, dimensions={0} | all-to-all | bytes 1048576 | tf_op jit(solution)/shard_map/all_to_all | solution.py:66
  176.3 0.6 reshape.150
  176.9 19.2 %fusion.2 = f32[2,2,64,2160]{3,2,1,0:T(8,128)} fusion(f32[2,2160,512]{2,1,0:T(8,128)} %param.12, f32[2,512,2,64]{3,2,1,0:T(2,128)S(1)} %reshape.150), kind=kOutput, calls=%fused_computation.3 | convolution fusion | flops 3397386240 | bytes 11583488 | tf_op jit(solution)/shard_map/mtsk,mdt->mskd/dot_general | solution.py:74
  196.3 61.3 %all-reduce.3.cloned.1.call-done = f32[2,2,64,2160]{3,2,1,0:T(8,128)} async-done(((f32[2,2,64,2160]{3,2,1,0:T(8,128)}), f32[2,2,64,2160]{3,2,1,0:T(8,128)}) %all-reduce.3.cloned.1.call-update) | async-done | bytes 2211856 | tf_op jit(solution)/shard_map/psum | solution.py:75
  257.6 1.6 multiply_reduce_fusion.1
  259.2 76.0 %all-reduce = (f32[64]{0:T(128)S(1)}, f32[64]{0:T(128)S(1)}) all-reduce(f32[64]{0:T(128)S(1)} %get-tuple-element.4, f32[64]{0:T(128)S(1)} %get-tuple-element.3), channel_id=1, replica_groups=mesh['order'=64,'lat'=4] {'order','lat'}, use_global_device_ids=true, to_apply=%region_1.0 | all-reduce | flops 128 | bytes 1024 | tf_op jit(solution)/shard_map/psum | solution.py:36
  335.1 2.5 multiply_reduce_fusion
  337.6 74.3 %psum.31 = f32[64]{0:T(128)S(1)} all-reduce(f32[64]{0:T(128)S(1)} %get-tuple-element.7), channel_id=1, replica_groups=mesh['order'=64,'lat'=4] {'order','lat'}, use_global_device_ids=true, to_apply=%region_6.7 | all-reduce | flops 64 | bytes 512 | tf_op jit(solution)/shard_map/psum | solution.py:81
  411.9 1.0 multiply_add_fusion
  (38 shorter events, 0.8 us)
Async XLA Ops:
  7.2 2.5 copy-start
  7.2 2.4 copy-start.10
  7.2 2.5 copy-start.11
  7.2 59.0 %all-gather.2.cloned.1.call-start = ((), (), s32[]{:S(2)}) async-start(), calls=%async_computation.2 | async-start | bytes 5529600 | tf_op jit(solution)/shard_map/all_gather | solution.py:37
  66.2 6.6 %copy-start.1 = (f32[2,2160,512]{2,1,0:T(8,128)S(1)}, f32[2,2160,512]{2,1,0:T(8,128)}, u32[]{:S(2)}) copy-start(f32[2,2160,512]{2,1,0:T(8,128)} %param.12) | copy-start | bytes 26542084
  72.7 20.8 %copy-start.7 = (f32[8,4320,1]{1,2,0:T(1,128)S(1)}, f32[8,4320,1]{1,2,0:T(1,128)}, u32[]{:S(2)}) copy-start(f32[8,4320,1]{1,2,0:T(1,128)} %get-tuple-element.11) | copy-start | bytes 414724
  72.8 20.8 %copy-start.8 = (s32[8,4320]{1,0:T(8,128)S(1)}, s32[8,4320]{1,0:T(8,128)}, u32[]{:S(2)}) copy-start(s32[8,4320]{1,0:T(8,128)} %param.15) | copy-start | bytes 414724
  82.5 28.5 %all-to-all-start = ((f32[2,512,128]{2,0,1:T(2,128)}), f32[2,512,128]{2,0,1:T(2,128)S(1)}, u32[]{:S(2)}, u32[]{:S(2)}) async-start(f32[2,512,128]{2,0,1:T(2,128)} %copy.22), calls=%async_computation | async-start | bytes 1048576 | tf_op jit(solution)/shard_map/all_to_all | solution.py:43
  93.3 164.3 %all-reduce.3.cloned.1.call-start = ((), (), s32[]{:S(2)}) async-start(), calls=%async_computation.3 | async-start | bytes 4456448 | tf_op jit(solution)/shard_map/psum | solution.py:75
  113.5 31.3 %copy-start.2 = (f32[1,128,4320]{1,2,0:T(8,128)S(1)}, f32[1,128,4320]{1,2,0:T(8,128)}, u32[]{:S(2)}) copy-start(f32[1,128,4320]{1,2,0:T(8,128)} %get-tuple-element.13) | copy-start | bytes 6635524
  196.2 61.4 %copy-start.3 = (f32[2,2,64,540]{3,2,1,0:T(8,128)S(1)}, f32[2,2,64,540]{3,2,1,0:T(8,128)}, u32[]{:S(2)}) copy-start(f32[2,2,64,540]{3,2,1,0:T(8,128)} %param.11) | copy-start | bytes 1658884
  196.2 61.4 %copy-start.4 = (f32[2,2,64,540]{3,2,1,0:T(8,128)S(1)}, f32[2,2,64,540]{3,2,1,0:T(8,128)}, u32[]{:S(2)}) copy-start(f32[2,2,64,540]{3,2,1,0:T(8,128)} %param.10) | copy-start | bytes 1658884
  196.2 61.4 %copy-start.9 = (f32[540]{0:T(1024)S(1)}, f32[540]{0:T(1024)}, u32[]{:S(2)}) copy-start(f32[540]{0:T(1024)} %param.17) | copy-start | bytes 6484
  196.2 138.9 %copy-start.6 = (f32[2,2,64,540]{3,2,1,0:T(8,128)S(1)}, f32[2,2,64,540]{3,2,1,0:T(8,128)}, u32[]{:S(2)}) copy-start(f32[2,2,64,540]{3,2,1,0:T(8,128)} %param.9) | copy-start | bytes 1658884
  337.6 75.3 %copy-start.5 = (f32[2,2,64,540]{3,2,1,0:T(8,128)}, f32[2,2,64,540]{3,2,1,0:T(8,128)S(1)}, u32[]{:S(2)}) copy-start(f32[2,2,64,540]{3,2,1,0:T(8,128)S(1)} %get-tuple-element.8) | copy-start | bytes 1658884
Sparse Core Ops, SparseCore 0:
  9.8 56.2 all-gather.1
  196.3 61.1 all-reduce.2
where the time goes:
time: 429 us; the launch traced here: 420 us
  blocking collectives  174 us (41%)
  waiting for transfers between devices  124 us (29%)
  matrix products  67.8 us (16%)
  other arithmetic  21.7 us (5%)
  between operations  14.5 us (3%)
  starting transfers between devices  11.1 us (3%)
  local copies, waits for them, and re-layouts  7.76 us (2%)
    psum x1, blocking collectives, shards(): norm_before = lax.psum(sample_sums(res_m * res_m), ('order', 'lat'))  76 us
    psum x1, blocking collectives, shards(): lax.psum(sample_sums(new_residual * new_residual), ('order', 'lat'))  74.3 us
    psum x1, waiting for transfers between devices, shards(): totals = lax.psum(band_part, 'lat')  61.3 us
    all_gather x1, waiting for transfers between devices, shards(): block_part = lax.all_gather(direction, 'lat', axis=3, tiled=True)  44.9 us
    dot_general x1, matrix products, shards(): surface = jnp.einsum('mrsk,sml->rkl', grid_in, harmonic, precision=highest)  31.3 us
    all_to_all x1, blocking collectives, shards(): lax.all_to_all(spectra.reshape(orders_all, rows_here, 2 * samples), 'orde...  23.3 us
    dot_general x1, matrix products, shards(): jnp.einsum('mtsk,mdt->mskd', returned, legendre, precision=highest)  19.2 us
    all_to_all x1, waiting for transfers between devices, shards(): lax.all_to_all(synthesis.reshape(m_local, band_rows, 2 * samples), 'order...  17.4 us
  transfers between devices with their start and end apart: 3, of which 3 were waited for; matrix products, arithmetic and copies ran while one was open for 3% of the time, Pallas kernels for 0%

commit v1 on v0

--- a/solution.py
+++ b/solution.py
@@ -34,7 +34,9 @@
     res_m = residual * own_valid
     dir_m = direction * own_valid
     norm_before = lax.psum(sample_sums(res_m * res_m), ("order", "lat"))
-    block_part = lax.all_gather(direction, "lat", axis=3, tiled=True)
+    block_part = jnp.concatenate(
+        lax.all_to_all(jnp.stack([direction] * lax.axis_size("lat")), "lat", 0, 0), axis=3
+    )
     degree_count = block_part.shape[3]
     in_block = jnp.arange(degree_count, dtype=jnp.int32)
     in_triangle = (in_block[None, :] >= my_orders[:, None]).astype(jnp.float32)

time: 429 us -> 412 us (0.960)
  waiting for transfers between devices: 124 us -> 96.8 us
  starting transfers between devices: 11.1 us -> 20.1 us
  local copies, waits for them, and re-layouts: 7.76 us -> 16.5 us
  other arithmetic: 21.7 us -> 15.1 us
    all_gather x1 -> x0, waiting for transfers between devices: 44.9 us -> none  [shards(): block_part = lax.all_gather(direction, 'lat', axis=3, tiled=True)]
    all_to_all x0 -> x1, waiting for transfers between devices: none -> 19 us  [shards(): lax.all_to_all(jnp.stack([direction] * lax.axis_size('lat')), 'lat', 0, 0)]
    reshape x0 -> x2, local copies, waits for them, and re-layouts: none -> 8.87 us  [shards(): jnp.concatenate(lax.all_to_all(jnp.stack([direction] * lax.axis_size('lat...]
    mul x1 -> x0, other arithmetic: 6.57 us -> none  [shards(): masked = block_part * in_triangle[:, None, None, :]]
    all_to_all x0 -> x1, starting transfers between devices: none -> 5.13 us  [shards(): lax.all_to_all(jnp.stack([direction] * lax.axis_size('lat')), 'lat', 0, 0)]
where the time goes in v1:
time: 412 us; the launch traced here: 405 us
  blocking collectives  174 us (42%)
  waiting for transfers between devices  96.8 us (23%)
  matrix products  68 us (17%)
  starting transfers between devices  20.1 us (5%)
  local copies, waits for them, and re-layouts  16.5 us (4%)
  other arithmetic  15.1 us (4%)
  between operations  14.4 us (3%)
    psum x1, blocking collectives, shards(): norm_before = lax.psum(sample_sums(res_m * res_m), ('order', 'lat'))  76 us
    psum x1, blocking collectives, shards(): lax.psum(sample_sums(new_residual * new_residual), ('order', 'lat'))  74.3 us
    psum x1, waiting for transfers between devices, shards(): totals = lax.psum(band_part, 'lat')  60.3 us
    dot_general x1, matrix products, shards(): surface = jnp.einsum('mrsk,sml->rkl', grid_in, harmonic, precision=highest)  31.3 us
    all_to_all x1, blocking collectives, shards(): lax.all_to_all(spectra.reshape(orders_all, rows_here, 2 * samples), 'orde...  23.3 us
    dot_general x1, matrix products, shards(): jnp.einsum('mtsk,mdt->mskd', returned, legendre, precision=highest)  19.3 us
    all_to_all x1, waiting for transfers between devices, shards(): lax.all_to_all(jnp.stack([direction] * lax.axis_size('lat')), 'lat', 0, 0)  19 us
    all_to_all x1, waiting for transfers between devices, shards(): lax.all_to_all(synthesis.reshape(m_local, band_rows, 2 * samples), 'order...  17.4 us
  transfers between devices with their start and end apart: 3, of which 3 were waited for; matrix products, arithmetic and copies ran while one was open for 3% of the time, Pallas kernels for 0%

profile of v1, /device:TPU:1, one launch (start us, length us, event | category | flops | bytes accessed | tf_op | source)
XLA Modules:
  0.0 404.5 jit_solution(17633733282573837712)
XLA Ops:
  7.2 2.9 stack.5
  10.0 5.1 %all-to-all-start = ((f32[4,2,2,64,540]{4,3,2,1,0:T(8,128)}), f32[4,2,2,64,540]{4,3,2,1,0:T(8,128)}, u32[]{:S(2)}, u32[]{:S(2)}) async-start(f32[4,2,2,64,540]{4,3,2,1,0:T(8,128)} %stack.5), calls=%async_computation | async-start | bytes 5242880 | tf_op jit(solution)/shard_map/all_to_all | solution.py:38
  15.2 0.7 fusion.11
  16.3 9.9 %fusion.17 = (f32[1,128,4320]{1,2,0:T(8,128)S(1)}, f32[1,128,4320]{1,2,0:T(8,128)}) fusion(s32[128]{0:T(128)S(1)} %copy-done.8), kind=kLoop, calls=%fused_computation.22 | loop fusion | flops 4976640 | bytes 4424192 | tf_op jit(solution)/shard_map/cos | solution.py:12
  26.2 19.0 %all-to-all-done = f32[4,2,2,64,540]{4,3,2,1,0:T(8,128)} async-done(((f32[4,2,2,64,540]{4,3,2,1,0:T(8,128)}), f32[4,2,2,64,540]{4,3,2,1,0:T(8,128)}, u32[]{:S(2)}, u32[]{:S(2)}) %all-to-all-start) | async-done | bytes 2211872 | tf_op jit(solution)/shard_map/all_to_all | solution.py:38
  45.2 4.9 %copy.29 = f32[2,2,64,4,540]{4,3,2,1,0:T(4,128)} copy(f32[2,2,64,4,540]{4,2,1,0,3:T(8,128)} %bitcast.2) | data formatting | bytes 4423680 | tf_op jit(solution)/shard_map/reshape | solution.py:37
  50.1 3.9 reshape.156
  54.1 8.9 %fusion.4 = f32[2,2,64,512]{3,2,1,0:T(8,128)S(1)} fusion(f32[2,2160,512]{2,1,0:T(8,128)} %param.12, f32[2,2,64,2160]{3,2,1,0:T(8,128)} %reshape.156, f32[2,2160]{1,0:T(2,128)S(1)} %compare_convert_fusion), kind=kOutput, calls=%fused_computation.5 | convolution fusion | flops 3397939200 | bytes 11600768 | tf_op jit(solution)/shard_map/mskd,mdt->mtsk/dot_general | solution.py:44
  63.0 1.0 copy.30
  64.0 14.8 %all-to-all-start.1 = ((f32[2,512,128]{2,0,1:T(2,128)}), f32[2,512,128]{2,0,1:T(2,128)S(1)}, u32[]{:S(2)}, u32[]{:S(2)}) async-start(f32[2,512,128]{2,0,1:T(2,128)} %copy.30), calls=%async_computation.1 | async-start | bytes 1048576 | tf_op jit(solution)/shard_map/all_to_all | solution.py:45
  79.1 17.4 %all-to-all-done.1 = f32[2,512,128]{2,0,1:T(2,128)S(1)} async-done(((f32[2,512,128]{2,0,1:T(2,128)}), f32[2,512,128]{2,0,1:T(2,128)S(1)}, u32[]{:S(2)}, u32[]{:S(2)}) %all-to-all-start.1) | async-done | bytes 524320 | tf_op jit(solution)/shard_map/all_to_all | solution.py:45
  96.5 0.8 copy.32
  97.3 1.6 reshape.158
  99.0 31.3 %fusion.8 = f32[8,64,4320,1]{2,1,3,0:T(8,128)S(1)} fusion(f32[1,128,4320]{1,2,0:T(8,128)} %get-tuple-element.13, f32[1,128,4320]{1,2,0:T(8,128)S(1)} %get-tuple-element.12, f32[128,8,2,64]{3,2,1,0:T(2,128)S(1)} %reshape.158), kind=kOutput, calls=%fused_computation.10 | convolution fusion | flops 6795878400 | bytes 13795328 | tf_op jit(solution)/shard_map/mrsk,sml->rkl/dot_general | solution.py:57
  130.3 7.8 %fusion.24 = f32[128,8,2,64]{0,3,1,2:T(8,128)S(1)} fusion(f32[8,64,4320,1]{2,1,3,0:T(8,128)S(1)} %fusion.8, f32[8,4320]{1,0:T(8,128)S(1)} %fusion.33, f32[1,128,4320]{1,2,0:T(8,128)S(1)} %copy-done.1, f32[1,128,4320]{1,2,0:T(8,128)S(1)} %get-tuple-element.12), kind=kOutput, calls=%fused_computation.25 | convolution fusion | flops 6798221312 | bytes 13933568 | tf_op jit(solution)/shard_map/rkl,sml->mrsk/dot_general | solution.py:65
  138.4 23.3 %all_to_all.35 = f32[128,8,128]{2,1,0:T(8,128)S(1)} all-to-all(f32[128,8,128]{2,1,0:T(8,128)S(1)} %copy.36), channel_id=1, replica_groups=mesh['order'=64,'lat'=4] {'order'}, dimensions={0} | all-to-all | bytes 1048576 | tf_op jit(solution)/shard_map/all_to_all | solution.py:68
  161.8 0.6 reshape.160
  162.4 19.3 %fusion.2 = f32[2,2,64,2160]{3,2,1,0:T(8,128)} fusion(f32[2,2160,512]{2,1,0:T(8,128)} %param.12, f32[2,512,2,64]{3,2,1,0:T(2,128)S(1)} %reshape.160), kind=kOutput, calls=%fused_computation.3 | convolution fusion | flops 3397386240 | bytes 11583488 | tf_op jit(solution)/shard_map/mtsk,mdt->mskd/dot_general | solution.py:76
  181.8 60.3 %all-reduce.3.cloned.1.call-done = f32[2,2,64,2160]{3,2,1,0:T(8,128)} async-done(((f32[2,2,64,2160]{3,2,1,0:T(8,128)}), f32[2,2,64,2160]{3,2,1,0:T(8,128)}) %all-reduce.3.cloned.1.call-update) | async-done | bytes 2211856 | tf_op jit(solution)/shard_map/psum | solution.py:77
  242.2 1.6 multiply_reduce_fusion.1
  243.7 76.0 %all-reduce = (f32[64]{0:T(128)S(1)}, f32[64]{0:T(128)S(1)}) all-reduce(f32[64]{0:T(128)S(1)} %get-tuple-element.4, f32[64]{0:T(128)S(1)} %get-tuple-element.3), channel_id=1, replica_groups=mesh['order'=64,'lat'=4] {'order','lat'}, use_global_device_ids=true, to_apply=%region_1.0 | all-reduce | flops 128 | bytes 1024 | tf_op jit(solution)/shard_map/psum | solution.py:36
  319.7 2.5 multiply_reduce_fusion
  322.2 74.3 %psum.31 = f32[64]{0:T(128)S(1)} all-reduce(f32[64]{0:T(128)S(1)} %get-tuple-element.7), channel_id=1, replica_groups=mesh['order'=64,'lat'=4] {'order','lat'}, use_global_device_ids=true, to_apply=%region_6.7 | all-reduce | flops 64 | bytes 512 | tf_op jit(solution)/shard_map/psum | solution.py:83
  396.5 1.0 multiply_add_fusion
  (34 shorter events, 1.1 us)
Async XLA Ops:
  7.2 8.0 %copy-start = (f32[16,2]{0,1:T(2,128)S(1)}, f32[16,2]{0,1:T(2,128)}, u32[]{:S(2)}) copy-start(f32[16,2]{0,1:T(2,128)} %param.16) | copy-start | bytes 388
  10.0 5.1 %copy-start.9 = (s32[8,4320]{1,0:T(8,128)S(1)}, s32[8,4320]{1,0:T(8,128)}, u32[]{:S(2)}) copy-start(s32[8,4320]{1,0:T(8,128)} %param.14) | copy-start | bytes 414724
  10.0 6.1 %copy-start.8 = (s32[128]{0:T(128)S(1)}, s32[128]{0:T(128)}, u32[]{:S(2)}) copy-start(s32[128]{0:T(128)} %param.13) | copy-start | bytes 1540
  10.0 35.2 %all-to-all-start = ((f32[4,2,2,64,540]{4,3,2,1,0:T(8,128)}), f32[4,2,2,64,540]{4,3,2,1,0:T(8,128)}, u32[]{:S(2)}, u32[]{:S(2)}) async-start(f32[4,2,2,64,540]{4,3,2,1,0:T(8,128)} %stack.5), calls=%async_computation | async-start | bytes 5242880 | tf_op jit(solution)/shard_map/all_to_all | solution.py:38
  54.1 24.9 %copy-start.6 = (s32[8,4320]{1,0:T(8,128)S(1)}, s32[8,4320]{1,0:T(8,128)}, u32[]{:S(2)}) copy-start(s32[8,4320]{1,0:T(8,128)} %param.15) | copy-start | bytes 414724
  64.0 32.5 %all-to-all-start.1 = ((f32[2,512,128]{2,0,1:T(2,128)}), f32[2,512,128]{2,0,1:T(2,128)S(1)}, u32[]{:S(2)}, u32[]{:S(2)}) async-start(f32[2,512,128]{2,0,1:T(2,128)} %copy.30), calls=%async_computation.1 | async-start | bytes 1048576 | tf_op jit(solution)/shard_map/all_to_all | solution.py:45
  78.8 163.4 %all-reduce.3.cloned.1.call-start = ((), (), s32[]{:S(2)}) async-start(), calls=%async_computation.3 | async-start | bytes 4456448 | tf_op jit(solution)/shard_map/psum | solution.py:77
  99.0 31.3 %copy-start.1 = (f32[1,128,4320]{1,2,0:T(8,128)S(1)}, f32[1,128,4320]{1,2,0:T(8,128)}, u32[]{:S(2)}) copy-start(f32[1,128,4320]{1,2,0:T(8,128)} %get-tuple-element.13) | copy-start | bytes 6635524
  181.7 60.5 %copy-start.2 = (f32[2,2,64,540]{3,2,1,0:T(8,128)S(1)}, f32[2,2,64,540]{3,2,1,0:T(8,128)}, u32[]{:S(2)}) copy-start(f32[2,2,64,540]{3,2,1,0:T(8,128)} %param.11) | copy-start | bytes 1658884
  181.7 60.5 %copy-start.3 = (f32[2,2,64,540]{3,2,1,0:T(8,128)S(1)}, f32[2,2,64,540]{3,2,1,0:T(8,128)}, u32[]{:S(2)}) copy-start(f32[2,2,64,540]{3,2,1,0:T(8,128)} %param.10) | copy-start | bytes 1658884
  181.7 60.5 %copy-start.7 = (f32[540]{0:T(1024)S(1)}, f32[540]{0:T(1024)}, u32[]{:S(2)}) copy-start(f32[540]{0:T(1024)} %param.17) | copy-start | bytes 6484
  181.7 138.0 %copy-start.5 = (f32[2,2,64,540]{3,2,1,0:T(8,128)S(1)}, f32[2,2,64,540]{3,2,1,0:T(8,128)}, u32[]{:S(2)}) copy-start(f32[2,2,64,540]{3,2,1,0:T(8,128)} %param.9) | copy-start | bytes 1658884
  322.2 75.3 %copy-start.4 = (f32[2,2,64,540]{3,2,1,0:T(8,128)}, f32[2,2,64,540]{3,2,1,0:T(8,128)S(1)}, u32[]{:S(2)}) copy-start(f32[2,2,64,540]{3,2,1,0:T(8,128)S(1)} %get-tuple-element.8) | copy-start | bytes 1658884
Sparse Core Ops, SparseCore 0:
  181.8 60.2 all-reduce.2
